TPU v7x, 256 devices: a whole 4x4x8 slice. The times are simulated.
256 devices in a mesh: req: 64 (over z, x, core), ffn: 4 (over y).
Axes of the slice: x: 4, y: 4, z: 8, core: 2. Of those that a mesh axis runs over, the one named last changes fastest.
Arguments:
- residual: bfloat16 [16384, 2048], P('req')
- queries: bfloat16 [16384, 4096], P('req', 'ffn')
- rotated_key_rows: bfloat16 [16384, 2048], P('req', 'ffn')
- values: bfloat16 [16384, 2048], P('req', 'ffn'), may hold values from -6 to 6
- req_start: int32 [16384], P('req'), may hold values from 0 to 16383, as said below
- head_sink_logit: float32 [32], P('ffn'), may hold values from 6 to 11
- out_proj: bfloat16 [4096, 2048], P('ffn', 'req'), may hold values from -0.25 to 0.25
- mid_gain: float32 [2048], replicated, may hold values from 0.1 to 1.9
- router_logits: float32 [16384, 8], P('req')
- routes: int32 [16384, 2], P('req'), may hold values from 0 to 63, as said below
- placement: int32 [64], replicated, may hold values from 0 to 7, as said below
- w_gate: bfloat16 [64, 2048, 3072], P('req', None, 'ffn'), as said below
- w_up: bfloat16 [64, 2048, 3072], P('req', None, 'ffn'), as said below
- w_down: bfloat16 [64, 2048, 3072], P('req', None, 'ffn'), as said below
Outputs:
- layer_out: bfloat16 [16384, 2048], P('req', 'ffn')
Inputs may be any that keep to these rules, and one draw needn't show every extreme that they name: req_start[p] is the first position of the request that holds position p; requests are runs of consecutive positions, each at most 8192 long, one is exactly 8192 long, and the last position is a request of one token. `routes`: the two entries of a token name indices that host different experts. Among the 512 entries of the tokens of one index of req, an index appears at most 10 times, and every index that hosts one certain expert appears exactly 10 times, in every such block. `placement`: every expert is hosted at one index or more. `w_gate`: rows k and m are equal where placement[k] == placement[m]. `w_up`: rows k and m are equal where placement[k] == placement[m]. `w_down`: rows k and m are equal where placement[k] == placement[m].
All inputs are finite; a program needn't handle non-finite values.
Results may differ from a plain program's by a relative error of at most 0.0075.
Values may be sent and summed in bfloat16 or wider, within the bound.
A program may use at most 128 MiB of HBM per device.

v0:
```python
import jax
import jax.numpy as jnp
from jax import lax
from jax.sharding import PartitionSpec as P

QUERY_HEADS = 32
KEY_VALUE_HEADS = 16
HEAD_SIZE = 128
EXPERTS = 8
EPS = 1e-06


def shifted(value, axis, steps):
    count = lax.axis_size(axis)
    initial, last = (max(0, -steps), min(count, count - steps))
    return lax.ppermute(value, axis, [(source, source + steps) for source in range(initial, last)])


def step_back(keys_in_block, values_in_block):
    return shifted((keys_in_block, values_in_block), "req", 1)


def per_device(
    residual,
    queries,
    rotated_key_rows,
    values,
    req_start,
    head_sink_logit,
    out_proj,
    mid_gain,
    router_logits,
    routes,
    placement,
    w_gate,
    w_up,
    w_down,
):
    tok_count = residual.shape[0]
    model_width = residual.shape[1]
    req_size = lax.axis_size("req")
    ffn_size = lax.axis_size("ffn")
    own_req = lax.axis_index("req")
    own_ffn = lax.axis_index("ffn")
    query_group_width = QUERY_HEADS // KEY_VALUE_HEADS
    kv_heads = rotated_key_rows.shape[1] // HEAD_SIZE
    quarter = model_width // ffn_size
    gate_mat = w_gate[0]
    up_mat = w_up[0]
    down_mat = w_down[0]
    shard_queries = queries.reshape(tok_count, kv_heads, query_group_width, HEAD_SIZE)
    local_keys = rotated_key_rows.reshape(tok_count, kv_heads, HEAD_SIZE)
    local_values = values.reshape(tok_count, kv_heads, HEAD_SIZE)
    win_span = min(16, req_size // 2)
    window = win_span * tok_count
    query_pos = own_req * tok_count + jnp.arange(tok_count, dtype=jnp.int32)
    logit_scale_factor = HEAD_SIZE ** (-0.5)

    def attend(carry_state, keys_in_block, values_in_block, key_first):
        running_max, row_total, weighted_value_sum = carry_state
        attention_logits = (
            jnp.einsum(
                "veck,uek->ecvu", shard_queries, keys_in_block, preferred_element_type=jnp.float32
            )
            * logit_scale_factor
        )
        key_pos = key_first + jnp.arange(keys_in_block.shape[0], dtype=jnp.int32)
        visible = (
            (key_pos[None, :] >= req_start[:, None])
            & (key_pos[None, :] <= query_pos[:, None])
            & (query_pos[:, None] - key_pos[None, :] < window)
        )
        attention_logits = jnp.where(visible[None, None], attention_logits, -jnp.inf)
        new_max = jnp.maximum(running_max, jnp.max(attention_logits, axis=-1))
        probs = jnp.exp(attention_logits - new_max[..., None])
        factor = jnp.exp(running_max - new_max)
        row_total = row_total * factor + jnp.sum(probs, axis=-1)
        weighted_value_sum = weighted_value_sum * factor[..., None] + jnp.einsum(
            "plyw,wpj->plyj",
            probs.astype(jnp.bfloat16),
            values_in_block,
            preferred_element_type=jnp.float32,
        )
        return (new_max, row_total, weighted_value_sum)

    initial_sink_logit = jnp.broadcast_to(
        head_sink_logit.reshape(kv_heads, query_group_width, 1),
        (kv_heads, query_group_width, tok_count),
    )
    carry_state = (
        initial_sink_logit,
        jnp.ones((kv_heads, query_group_width, tok_count), jnp.float32),
        jnp.zeros((kv_heads, query_group_width, tok_count, HEAD_SIZE), jnp.float32),
    )
    carry_state = attend(carry_state, local_keys, local_values, own_req * tok_count)
    pair_count = win_span // 2

    def pair_step(step_idx, loop_carry):
        folded, near_keys, near_values = loop_carry
        mid_keys, mid_values = step_back(near_keys, near_values)
        far_keys, far_values = step_back(mid_keys, mid_values)
        key_first = (own_req - 2 * step_idx - 2) * tok_count
        folded = attend(
            folded,
            jnp.concatenate([far_keys, mid_keys], 0),
            jnp.concatenate([far_values, mid_values], 0),
            key_first,
        )
        return (folded, far_keys, far_values)

    carry_state, unused_keys, unused_values = lax.fori_loop(
        0, pair_count, pair_step, (carry_state, local_keys, local_values)
    )
    running_max, row_total, weighted_value_sum = carry_state
    attended = (weighted_value_sum / row_total[..., None]).astype(jnp.bfloat16)
    flat_attended = jnp.transpose(attended, (2, 0, 1, 3)).reshape(tok_count, -1)
    proj = jnp.dot(
        flat_attended,
        lax.all_gather(out_proj, "req", axis=1, tiled=True),
        preferred_element_type=jnp.float32,
    )
    summed = lax.psum(proj.astype(jnp.bfloat16), "ffn").astype(jnp.float32)
    hidden_state = residual.astype(jnp.float32) + summed
    mean_sq = jnp.mean(hidden_state * hidden_state, axis=1, keepdims=True)
    normed = (hidden_state * lax.rsqrt(mean_sq + EPS) * mid_gain).astype(jnp.bfloat16)
    own_hidden = lax.dynamic_slice_in_dim(hidden_state, own_ffn * quarter, quarter, 1)
    capacity = 5 * tok_count // (2 * req_size)
    flat_routes = routes.reshape(-1)
    slot_iota = jnp.arange(req_size, dtype=jnp.int32)
    dest_hot = (flat_routes[:, None] == slot_iota[None, :]).astype(jnp.int32)
    slot_depth = jnp.sum((jnp.cumsum(dest_hot, axis=0) - dest_hot) * dest_hot, axis=1)
    slot_index = flat_routes * capacity + slot_depth
    row_tokens = jnp.arange(2 * tok_count, dtype=jnp.int32) // 2
    send_rows = (
        jnp.zeros((req_size * capacity, model_width), jnp.bfloat16)
        .at[slot_index]
        .set(normed[row_tokens])
    )
    send_rows = send_rows.reshape(req_size, capacity, model_width)
    arrived = lax.all_to_all(send_rows, "req", split_axis=0, concat_axis=0, tiled=True)
    flat_rows = arrived.reshape(-1, model_width)
    gate_val = jnp.dot(flat_rows, gate_mat, preferred_element_type=jnp.float32)
    up_val = jnp.dot(flat_rows, up_mat, preferred_element_type=jnp.float32)
    activated = (jax.nn.silu(gate_val) * up_val).astype(jnp.bfloat16)
    partial_out = lax.dot_general(
        activated, down_mat, (((1,), (1,)), ((), ())), preferred_element_type=jnp.float32
    )
    partial_rows = partial_out.astype(jnp.bfloat16).reshape(
        arrived.shape[0], arrived.shape[1], model_width
    )
    returned_parts = lax.all_to_all(
        lax.all_to_all(partial_rows[None], "req", split_axis=1, concat_axis=1, tiled=True),
        "ffn",
        split_axis=3,
        concat_axis=0,
        tiled=True,
    )
    returned = jnp.sum(returned_parts.astype(jnp.float32), axis=0)
    expert_of = jnp.sum(dest_hot * placement[None, :], axis=1).reshape(tok_count, 2)
    expert_hot = (
        expert_of[:, :, None] == jnp.arange(EXPERTS, dtype=jnp.int32)[None, None, :]
    ).astype(jnp.float32)
    chosen = jnp.sum(router_logits[:, None, :] * expert_hot, axis=2)
    logit_peak = jnp.max(chosen, axis=1, keepdims=True)
    exp_logits = jnp.exp(chosen - logit_peak)
    gate_weights = exp_logits / jnp.sum(exp_logits, axis=1, keepdims=True)
    picked = returned.reshape(req_size * capacity, quarter)[slot_index].reshape(
        tok_count, 2, quarter
    )
    mixture = jnp.sum(picked * gate_weights[:, :, None], axis=1)
    return (own_hidden + mixture).astype(jnp.bfloat16)


def solution(mesh):
    in_specs = (
        P("req", None),
        P("req", "ffn"),
        P("req", "ffn"),
        P("req", "ffn"),
        P("req"),
        P("ffn"),
        P("ffn", "req"),
        P(),
        P("req", None),
        P("req", None),
        P(),
        P("req", None, "ffn"),
        P("req", None, "ffn"),
        P("req", None, "ffn"),
    )
    out_specs = P("req", "ffn")
    return jax.shard_map(
        per_device, mesh=mesh, in_specs=in_specs, out_specs=out_specs, check_vma=False
    )
```

profile of v0, /device:TPU:32, one launch (start us, length us, event | category | flops | bytes accessed | tf_op | source)
XLA Modules:
  0.0 686.9 jit_solution(4302674995303318617)
XLA Ops:
  25.7 217.4 %while.24 = (s32[]{:T(128)}, f32[4,2,256]{2,1,0:T(2,128)S(1)}, f32[4,2,256]{2,1,0:T(2,128)S(1)}, f32[4,2,256,128]{3,2,1,0:T(8,128)}, bf16[256,4,128]{2,0,1:T(8,1...) while((s32[]{:T(128)}, f32[4,2,256]{2,1,0:T(2,128)S(1)}, ...), condition=%wide.region_5.6_spmd.clone, body=%wide.region_2.5_spmd.clone.sunk | while | flops 551817984 | bytes 30547376 | solution.py:111
  41.2 5.1 collective-permute-done.1
  57.1 6.0 collective-permute-done
  69.4 5.7 collective-permute-done.1
  87.7 6.0 collective-permute-done
  98.5 5.3 collective-permute-done.1
  114.2 6.0 collective-permute-done
  125.0 5.3 collective-permute-done.1
  140.8 6.0 collective-permute-done
  151.5 5.3 collective-permute-done.1
  167.3 6.0 collective-permute-done
  178.1 5.3 collective-permute-done.1
  193.9 6.0 collective-permute-done
  204.6 5.3 collective-permute-done.1
  220.4 6.0 collective-permute-done
  231.2 5.3 collective-permute-done.1
  254.9 69.6 %all-reduce.2.cloned.1.call-done = bf16[256,2048]{1,0:T(8,128)(2,1)} async-done(((bf16[256,2048]{1,0:T(8,128)(2,1)}), bf16[256,2048]{1,0:T(8,128)(2,1)}) %all-reduce.2.cloned.1.call-update) | async-done | bytes 1048592 | tf_op jit(solution)/shard_map/psum | solution.py:122
  329.4 11.3 %scatter_custom_fusion = bf16[640,2048]{1,0:T(8,128)(2,1)} fusion(s32[512]{0:T(512)S(1)} %bitcast.136, bf16[256,2048]{1,0:T(8,128)(2,1)} %multiply_convert_fusion, s32[1024]{0:T(1024)S(1)} %pad_clamp_fusion.1, bf16[]{:T(256)} %constant.128.clone.1), kind=kCustom, calls=%fused_computation.40 | custom fusion | bytes 2621952 | tf_op jit(solution)/shard_map/scatter | solution.py:137
  340.7 5.4 reshape.364
  346.1 106.1 %all_to_all.19 = bf16[64,10,2048]{2,1,0:T(8,128)(2,1)} all-to-all(bf16[64,10,2048]{2,1,0:T(8,128)(2,1)} %reshape.364), channel_id=1, replica_groups=mesh['req'=64,'ffn'=4] {'req'}, dimensions={0} | all-to-all | bytes 5242880 | tf_op jit(solution)/shard_map/all_to_all | solution.py:140
  452.2 5.5 reshape.365
  457.7 6.2 fusion.27
  463.9 9.7 %convolution_convert_fusion = bf16[640,2048]{1,0:T(8,128)(2,1)} fusion(bf16[1,2048,768]{2,1,0:T(8,128)(2,1)S(1)} %copy-done, f32[640,768]{1,0:T(8,128)} %fusion.27, bf16[640,2048]{1,0:T(8,128)(2,1)} %reshape.365, bf16[1,2048,768]{2,1,0:T(8,128)(2,1)} %param.28), kind=kOutput, calls=%fused_computation.32 | convolution fusion | flops 4030791680 | bytes 13500416 | tf_op jit(solution)/shard_map/dot_general | solution.py:145
  473.6 5.4 broadcast_in_dim_reshape.2
  478.9 101.8 %all_to_all.20 = bf16[1,64,10,2048]{3,2,0,1:T(8,128)(2,1)} all-to-all(bf16[1,64,10,2048]{3,2,0,1:T(8,128)(2,1)} %bitcast.121), channel_id=1, replica_groups=mesh['req'=64,'ffn'=4] {'req'}, dimensions={1} | all-to-all | bytes 5242880 | tf_op jit(solution)/shard_map/all_to_all | solution.py:152
  580.8 14.3 %copy.117 = bf16[1,64,10,2048]{1,2,0,3:T(8,128)(2,1)} copy(bf16[1,64,10,2048]{3,2,0,1:T(8,128)(2,1)} %all_to_all.20) | data formatting | bytes 5242880 | tf_op jit(solution)/shard_map/all_to_all | solution.py:152
  595.1 7.5 %reshape.404 = bf16[4,2,163840]{2,1,0:T(2,128)(2,1)} reshape(bf16[2048,1,10,64]{3,2,1,0:T(8,128)(2,1)} %bitcast.119) | data formatting | bytes 5242880
  607.4 31.6 %all-to-all-done.2 = bf16[4,2,163840]{2,1,0:T(2,128)(2,1)S(1)} async-done(((bf16[4,2,163840]{2,1,0:T(2,128)(2,1)}), bf16[4,2,163840]{2,1,0:T(2,128)(2,1)S(1)}, u32[]{:S(2)}, u32[]{:S(2)}) %all-to-all-start.2) | async-done | bytes 2621472 | tf_op jit(solution)/shard_map/all_to_all | solution.py:151
  638.9 5.8 reshape.405
  644.8 7.9 %copy.118 = bf16[1,64,10,2048]{3,1,2,0:T(8,128)(2,1)S(1)} copy(bf16[1,64,10,2048]{1,2,0,3:T(8,128)(2,1)} %bitcast.120) | data formatting | bytes 5242880 | tf_op jit(solution)/shard_map/all_to_all | solution.py:151
  652.6 5.5 reshape.368
  658.1 6.8 reduce_sum.94
  (246 shorter events, 186.9 us)
Async XLA Ops:
  6.5 241.2 %all-gather.2.cloned.1.call-start = ((), (), s32[]{:S(2)}) async-start(), calls=%async_computation.3 | async-start | bytes 4259840 | tf_op jit(solution)/shard_map/all_gather | solution.py:119
  7.3 317.2 %all-reduce.2.cloned.1.call-start = ((), (), s32[]{:S(2)}) async-start(), calls=%async_computation.4 | async-start | bytes 2097152 | tf_op jit(solution)/shard_map/psum | solution.py:122
  25.7 10.2 %collective-permute-start = (bf16[256,4,128]{2,0,1:T(8,128)(2,1)S(1)}, bf16[256,4,128]{2,0,1:T(8,128)(2,1)}, u32[]{:S(2)}, u32[]{:S(2)}) collective-permute-start(bf16[256,4,128]{2,0,1:T(8,128)(2,1)S(1)} %get-tuple-element.446), channel_id=1, source_target_pairs={{0,4},{4,8},{8,12},{12,16},{16,20},{20,24},{24,28},{28,32},{32,36}... | collective-permute-start | bytes 786440 | tf_op jit(solution)/shard_map/while/body/eval_jaxpr/ppermute | solution.py:16
  27.6 11.7 %collective-permute-start.2 = (bf16[256,4,128]{2,0,1:T(8,128)(2,1)}, bf16[256,4,128]{2,0,1:T(8,128)(2,1)}, u32[]{:S(2)}, u32[]{:S(2)}) collective-permute-start(bf16[256,4,128]{2,0,1:T(8,128)(2,1)} %get-tuple-element.447), channel_id=1, source_target_pairs={{0,4},{4,8},{8,12},{12,16},{16,20},{20,24},{24,28},{28,32},{32,36}... | collective-permute-start | bytes 786440 | tf_op jit(solution)/shard_map/while/body/eval_jaxpr/ppermute | solution.py:16
  35.9 10.4 %collective-permute-start.1 = (bf16[256,4,128]{2,0,1:T(8,128)(2,1)}, bf16[256,4,128]{2,0,1:T(8,128)(2,1)S(1)}, u32[]{:S(2)}, u32[]{:S(2)}) collective-permute-start(bf16[256,4,128]{2,0,1:T(8,128)(2,1)} %collective-permute-done), channel_id=1, source_target_pairs={{0,4},{4,8},{8,12},{12,16},{16,20},{20,24},{24,28},{28,32},{32,36}... | collective-permute-start | bytes 786440 | tf_op jit(solution)/shard_map/while/body/eval_jaxpr/ppermute | solution.py:16
  39.3 10.3 %collective-permute-start.3 = (bf16[256,4,128]{2,0,1:T(8,128)(2,1)}, bf16[256,4,128]{2,0,1:T(8,128)(2,1)S(1)}, u32[]{:S(2)}, u32[]{:S(2)}) collective-permute-start(bf16[256,4,128]{2,0,1:T(8,128)(2,1)} %collective-permute-done.2), channel_id=1, source_target_pairs={{0,4},{4,8},{8,12},{12,16},{16,20},{20,24},{24,28},{28,32},{32,36}... | collective-permute-start | bytes 786440 | tf_op jit(solution)/shard_map/while/body/eval_jaxpr/ppermute | solution.py:16
  53.3 9.9 %collective-permute-start = (bf16[256,4,128]{2,0,1:T(8,128)(2,1)S(1)}, bf16[256,4,128]{2,0,1:T(8,128)(2,1)}, u32[]{:S(2)}, u32[]{:S(2)}) collective-permute-start(bf16[256,4,128]{2,0,1:T(8,128)(2,1)S(1)} %get-tuple-element.446), channel_id=1, source_target_pairs={{0,4},{4,8},{8,12},{12,16},{16,20},{20,24},{24,28},{28,32},{32,36}... | collective-permute-start | bytes 786440 | tf_op jit(solution)/shard_map/while/body/eval_jaxpr/ppermute | solution.py:16
  55.2 12.3 %collective-permute-start.2 = (bf16[256,4,128]{2,0,1:T(8,128)(2,1)}, bf16[256,4,128]{2,0,1:T(8,128)(2,1)}, u32[]{:S(2)}, u32[]{:S(2)}) collective-permute-start(bf16[256,4,128]{2,0,1:T(8,128)(2,1)} %get-tuple-element.447), channel_id=1, source_target_pairs={{0,4},{4,8},{8,12},{12,16},{16,20},{20,24},{24,28},{28,32},{32,36}... | collective-permute-start | bytes 786440 | tf_op jit(solution)/shard_map/while/body/eval_jaxpr/ppermute | solution.py:16
  63.2 11.9 %collective-permute-start.1 = (bf16[256,4,128]{2,0,1:T(8,128)(2,1)}, bf16[256,4,128]{2,0,1:T(8,128)(2,1)S(1)}, u32[]{:S(2)}, u32[]{:S(2)}) collective-permute-start(bf16[256,4,128]{2,0,1:T(8,128)(2,1)} %collective-permute-done), channel_id=1, source_target_pairs={{0,4},{4,8},{8,12},{12,16},{16,20},{20,24},{24,28},{28,32},{32,36}... | collective-permute-start | bytes 786440 | tf_op jit(solution)/shard_map/while/body/eval_jaxpr/ppermute | solution.py:16
  67.5 12.7 %collective-permute-start.3 = (bf16[256,4,128]{2,0,1:T(8,128)(2,1)}, bf16[256,4,128]{2,0,1:T(8,128)(2,1)S(1)}, u32[]{:S(2)}, u32[]{:S(2)}) collective-permute-start(bf16[256,4,128]{2,0,1:T(8,128)(2,1)} %collective-permute-done.2), channel_id=1, source_target_pairs={{0,4},{4,8},{8,12},{12,16},{16,20},{20,24},{24,28},{28,32},{32,36}... | collective-permute-start | bytes 786440 | tf_op jit(solution)/shard_map/while/body/eval_jaxpr/ppermute | solution.py:16
  83.8 9.9 %collective-permute-start = (bf16[256,4,128]{2,0,1:T(8,128)(2,1)S(1)}, bf16[256,4,128]{2,0,1:T(8,128)(2,1)}, u32[]{:S(2)}, u32[]{:S(2)}) collective-permute-start(bf16[256,4,128]{2,0,1:T(8,128)(2,1)S(1)} %get-tuple-element.446), channel_id=1, source_target_pairs={{0,4},{4,8},{8,12},{12,16},{16,20},{20,24},{24,28},{28,32},{32,36}... | collective-permute-start | bytes 786440 | tf_op jit(solution)/shard_map/while/body/eval_jaxpr/ppermute | solution.py:16
  85.7 10.8 %collective-permute-start.2 = (bf16[256,4,128]{2,0,1:T(8,128)(2,1)}, bf16[256,4,128]{2,0,1:T(8,128)(2,1)}, u32[]{:S(2)}, u32[]{:S(2)}) collective-permute-start(bf16[256,4,128]{2,0,1:T(8,128)(2,1)} %get-tuple-element.447), channel_id=1, source_target_pairs={{0,4},{4,8},{8,12},{12,16},{16,20},{20,24},{24,28},{28,32},{32,36}... | collective-permute-start | bytes 786440 | tf_op jit(solution)/shard_map/while/body/eval_jaxpr/ppermute | solution.py:16
  93.7 10.0 %collective-permute-start.1 = (bf16[256,4,128]{2,0,1:T(8,128)(2,1)}, bf16[256,4,128]{2,0,1:T(8,128)(2,1)S(1)}, u32[]{:S(2)}, u32[]{:S(2)}) collective-permute-start(bf16[256,4,128]{2,0,1:T(8,128)(2,1)} %collective-permute-done), channel_id=1, source_target_pairs={{0,4},{4,8},{8,12},{12,16},{16,20},{20,24},{24,28},{28,32},{32,36}... | collective-permute-start | bytes 786440 | tf_op jit(solution)/shard_map/while/body/eval_jaxpr/ppermute | solution.py:16
  96.5 10.0 %collective-permute-start.3 = (bf16[256,4,128]{2,0,1:T(8,128)(2,1)}, bf16[256,4,128]{2,0,1:T(8,128)(2,1)S(1)}, u32[]{:S(2)}, u32[]{:S(2)}) collective-permute-start(bf16[256,4,128]{2,0,1:T(8,128)(2,1)} %collective-permute-done.2), channel_id=1, source_target_pairs={{0,4},{4,8},{8,12},{12,16},{16,20},{20,24},{24,28},{28,32},{32,36}... | collective-permute-start | bytes 786440 | tf_op jit(solution)/shard_map/while/body/eval_jaxpr/ppermute | solution.py:16
  110.4 9.9 %collective-permute-start = (bf16[256,4,128]{2,0,1:T(8,128)(2,1)S(1)}, bf16[256,4,128]{2,0,1:T(8,128)(2,1)}, u32[]{:S(2)}, u32[]{:S(2)}) collective-permute-start(bf16[256,4,128]{2,0,1:T(8,128)(2,1)S(1)} %get-tuple-element.446), channel_id=1, source_target_pairs={{0,4},{4,8},{8,12},{12,16},{16,20},{20,24},{24,28},{28,32},{32,36}... | collective-permute-start | bytes 786440 | tf_op jit(solution)/shard_map/while/body/eval_jaxpr/ppermute | solution.py:16
  112.3 10.8 %collective-permute-start.2 = (bf16[256,4,128]{2,0,1:T(8,128)(2,1)}, bf16[256,4,128]{2,0,1:T(8,128)(2,1)}, u32[]{:S(2)}, u32[]{:S(2)}) collective-permute-start(bf16[256,4,128]{2,0,1:T(8,128)(2,1)} %get-tuple-element.447), channel_id=1, source_target_pairs={{0,4},{4,8},{8,12},{12,16},{16,20},{20,24},{24,28},{28,32},{32,36}... | collective-permute-start | bytes 786440 | tf_op jit(solution)/shard_map/while/body/eval_jaxpr/ppermute | solution.py:16
  120.3 10.0 %collective-permute-start.1 = (bf16[256,4,128]{2,0,1:T(8,128)(2,1)}, bf16[256,4,128]{2,0,1:T(8,128)(2,1)S(1)}, u32[]{:S(2)}, u32[]{:S(2)}) collective-permute-start(bf16[256,4,128]{2,0,1:T(8,128)(2,1)} %collective-permute-done), channel_id=1, source_target_pairs={{0,4},{4,8},{8,12},{12,16},{16,20},{20,24},{24,28},{28,32},{32,36}... | collective-permute-start | bytes 786440 | tf_op jit(solution)/shard_map/while/body/eval_jaxpr/ppermute | solution.py:16
  123.1 10.0 %collective-permute-start.3 = (bf16[256,4,128]{2,0,1:T(8,128)(2,1)}, bf16[256,4,128]{2,0,1:T(8,128)(2,1)S(1)}, u32[]{:S(2)}, u32[]{:S(2)}) collective-permute-start(bf16[256,4,128]{2,0,1:T(8,128)(2,1)} %collective-permute-done.2), channel_id=1, source_target_pairs={{0,4},{4,8},{8,12},{12,16},{16,20},{20,24},{24,28},{28,32},{32,36}... | collective-permute-start | bytes 786440 | tf_op jit(solution)/shard_map/while/body/eval_jaxpr/ppermute | solution.py:16
  136.9 9.9 %collective-permute-start = (bf16[256,4,128]{2,0,1:T(8,128)(2,1)S(1)}, bf16[256,4,128]{2,0,1:T(8,128)(2,1)}, u32[]{:S(2)}, u32[]{:S(2)}) collective-permute-start(bf16[256,4,128]{2,0,1:T(8,128)(2,1)S(1)} %get-tuple-element.446), channel_id=1, source_target_pairs={{0,4},{4,8},{8,12},{12,16},{16,20},{20,24},{24,28},{28,32},{32,36}... | collective-permute-start | bytes 786440 | tf_op jit(solution)/shard_map/while/body/eval_jaxpr/ppermute | solution.py:16
  138.8 10.8 %collective-permute-start.2 = (bf16[256,4,128]{2,0,1:T(8,128)(2,1)}, bf16[256,4,128]{2,0,1:T(8,128)(2,1)}, u32[]{:S(2)}, u32[]{:S(2)}) collective-permute-start(bf16[256,4,128]{2,0,1:T(8,128)(2,1)} %get-tuple-element.447), channel_id=1, source_target_pairs={{0,4},{4,8},{8,12},{12,16},{16,20},{20,24},{24,28},{28,32},{32,36}... | collective-permute-start | bytes 786440 | tf_op jit(solution)/shard_map/while/body/eval_jaxpr/ppermute | solution.py:16
  146.8 10.0 %collective-permute-start.1 = (bf16[256,4,128]{2,0,1:T(8,128)(2,1)}, bf16[256,4,128]{2,0,1:T(8,128)(2,1)S(1)}, u32[]{:S(2)}, u32[]{:S(2)}) collective-permute-start(bf16[256,4,128]{2,0,1:T(8,128)(2,1)} %collective-permute-done), channel_id=1, source_target_pairs={{0,4},{4,8},{8,12},{12,16},{16,20},{20,24},{24,28},{28,32},{32,36}... | collective-permute-start | bytes 786440 | tf_op jit(solution)/shard_map/while/body/eval_jaxpr/ppermute | solution.py:16
  149.6 10.0 %collective-permute-start.3 = (bf16[256,4,128]{2,0,1:T(8,128)(2,1)}, bf16[256,4,128]{2,0,1:T(8,128)(2,1)S(1)}, u32[]{:S(2)}, u32[]{:S(2)}) collective-permute-start(bf16[256,4,128]{2,0,1:T(8,128)(2,1)} %collective-permute-done.2), channel_id=1, source_target_pairs={{0,4},{4,8},{8,12},{12,16},{16,20},{20,24},{24,28},{28,32},{32,36}... | collective-permute-start | bytes 786440 | tf_op jit(solution)/shard_map/while/body/eval_jaxpr/ppermute | solution.py:16
  165.4 10.8 %collective-permute-start.2 = (bf16[256,4,128]{2,0,1:T(8,128)(2,1)}, bf16[256,4,128]{2,0,1:T(8,128)(2,1)}, u32[]{:S(2)}, u32[]{:S(2)}) collective-permute-start(bf16[256,4,128]{2,0,1:T(8,128)(2,1)} %get-tuple-element.447), channel_id=1, source_target_pairs={{0,4},{4,8},{8,12},{12,16},{16,20},{20,24},{24,28},{28,32},{32,36}... | collective-permute-start | bytes 786440 | tf_op jit(solution)/shard_map/while/body/eval_jaxpr/ppermute | solution.py:16
  173.4 10.0 %collective-permute-start.1 = (bf16[256,4,128]{2,0,1:T(8,128)(2,1)}, bf16[256,4,128]{2,0,1:T(8,128)(2,1)S(1)}, u32[]{:S(2)}, u32[]{:S(2)}) collective-permute-start(bf16[256,4,128]{2,0,1:T(8,128)(2,1)} %collective-permute-done), channel_id=1, source_target_pairs={{0,4},{4,8},{8,12},{12,16},{16,20},{20,24},{24,28},{28,32},{32,36}... | collective-permute-start | bytes 786440 | tf_op jit(solution)/shard_map/while/body/eval_jaxpr/ppermute | solution.py:16
  176.2 10.0 %collective-permute-start.3 = (bf16[256,4,128]{2,0,1:T(8,128)(2,1)}, bf16[256,4,128]{2,0,1:T(8,128)(2,1)S(1)}, u32[]{:S(2)}, u32[]{:S(2)}) collective-permute-start(bf16[256,4,128]{2,0,1:T(8,128)(2,1)} %collective-permute-done.2), channel_id=1, source_target_pairs={{0,4},{4,8},{8,12},{12,16},{16,20},{20,24},{24,28},{28,32},{32,36}... | collective-permute-start | bytes 786440 | tf_op jit(solution)/shard_map/while/body/eval_jaxpr/ppermute | solution.py:16
  191.9 10.8 %collective-permute-start.2 = (bf16[256,4,128]{2,0,1:T(8,128)(2,1)}, bf16[256,4,128]{2,0,1:T(8,128)(2,1)}, u32[]{:S(2)}, u32[]{:S(2)}) collective-permute-start(bf16[256,4,128]{2,0,1:T(8,128)(2,1)} %get-tuple-element.447), channel_id=1, source_target_pairs={{0,4},{4,8},{8,12},{12,16},{16,20},{20,24},{24,28},{28,32},{32,36}... | collective-permute-start | bytes 786440 | tf_op jit(solution)/shard_map/while/body/eval_jaxpr/ppermute | solution.py:16
  199.9 10.0 %collective-permute-start.1 = (bf16[256,4,128]{2,0,1:T(8,128)(2,1)}, bf16[256,4,128]{2,0,1:T(8,128)(2,1)S(1)}, u32[]{:S(2)}, u32[]{:S(2)}) collective-permute-start(bf16[256,4,128]{2,0,1:T(8,128)(2,1)} %collective-permute-done), channel_id=1, source_target_pairs={{0,4},{4,8},{8,12},{12,16},{16,20},{20,24},{24,28},{28,32},{32,36}... | collective-permute-start | bytes 786440 | tf_op jit(solution)/shard_map/while/body/eval_jaxpr/ppermute | solution.py:16
  202.7 10.0 %collective-permute-start.3 = (bf16[256,4,128]{2,0,1:T(8,128)(2,1)}, bf16[256,4,128]{2,0,1:T(8,128)(2,1)S(1)}, u32[]{:S(2)}, u32[]{:S(2)}) collective-permute-start(bf16[256,4,128]{2,0,1:T(8,128)(2,1)} %collective-permute-done.2), channel_id=1, source_target_pairs={{0,4},{4,8},{8,12},{12,16},{16,20},{20,24},{24,28},{28,32},{32,36}... | collective-permute-start | bytes 786440 | tf_op jit(solution)/shard_map/while/body/eval_jaxpr/ppermute | solution.py:16
  218.5 10.8 %collective-permute-start.2 = (bf16[256,4,128]{2,0,1:T(8,128)(2,1)}, bf16[256,4,128]{2,0,1:T(8,128)(2,1)}, u32[]{:S(2)}, u32[]{:S(2)}) collective-permute-start(bf16[256,4,128]{2,0,1:T(8,128)(2,1)} %get-tuple-element.447), channel_id=1, source_target_pairs={{0,4},{4,8},{8,12},{12,16},{16,20},{20,24},{24,28},{28,32},{32,36}... | collective-permute-start | bytes 786440 | tf_op jit(solution)/shard_map/while/body/eval_jaxpr/ppermute | solution.py:16
  226.5 10.0 %collective-permute-start.1 = (bf16[256,4,128]{2,0,1:T(8,128)(2,1)}, bf16[256,4,128]{2,0,1:T(8,128)(2,1)S(1)}, u32[]{:S(2)}, u32[]{:S(2)}) collective-permute-start(bf16[256,4,128]{2,0,1:T(8,128)(2,1)} %collective-permute-done), channel_id=1, source_target_pairs={{0,4},{4,8},{8,12},{12,16},{16,20},{20,24},{24,28},{28,32},{32,36}... | collective-permute-start | bytes 786440 | tf_op jit(solution)/shard_map/while/body/eval_jaxpr/ppermute | solution.py:16
  229.3 10.0 %collective-permute-start.3 = (bf16[256,4,128]{2,0,1:T(8,128)(2,1)}, bf16[256,4,128]{2,0,1:T(8,128)(2,1)S(1)}, u32[]{:S(2)}, u32[]{:S(2)}) collective-permute-start(bf16[256,4,128]{2,0,1:T(8,128)(2,1)} %collective-permute-done.2), channel_id=1, source_target_pairs={{0,4},{4,8},{8,12},{12,16},{16,20},{20,24},{24,28},{28,32},{32,36}... | collective-permute-start | bytes 786440 | tf_op jit(solution)/shard_map/while/body/eval_jaxpr/ppermute | solution.py:16
  602.6 36.3 %all-to-all-start.2 = ((bf16[4,2,163840]{2,1,0:T(2,128)(2,1)}), bf16[4,2,163840]{2,1,0:T(2,128)(2,1)S(1)}, u32[]{:S(2)}, u32[]{:S(2)}) async-start(bf16[4,2,163840]{2,1,0:T(2,128)(2,1)} %reshape.404), calls=%async_computation.2 | async-start | bytes 5242880 | tf_op jit(solution)/shard_map/all_to_all | solution.py:151
  (38 other events, 655.5 us)
Sparse Core Ops, SparseCore 0:
  10.1 83.0 all-gather.1
  252.6 71.8 all-reduce.1
where the time goes:
time: 696 us; the launch traced here: 687 us
  blocking collectives  208 us (30%)
  waiting for transfers between devices  201 us (29%)
  local copies, waits for them, and re-layouts  105 us (15%)
  starting transfers between devices  67.1 us (10%)
  matrix products  60.8 us (9%)
  other arithmetic  29.8 us (4%)
  between operations  13.9 us (2%)
    all_to_all x1, blocking collectives, per_device(): lax.all_to_all(send_rows, 'req', split_axis=0, concat_axis=0, tiled=True)  106 us
    all_to_all x1, blocking collectives, per_device(): lax.all_to_all(partial_rows[None], 'req', split_axis=1, concat_axis=1, ti...  102 us
    ppermute x32, waiting for transfers between devices, shifted(): lax.ppermute(value, axis, [(source, source + steps) for source in range(i...  99.5 us
    psum x1, waiting for transfers between devices, per_device(): summed = lax.psum(proj.astype(jnp.bfloat16), 'ffn').astype(jnp.float32)  69.6 us
    ppermute x32, starting transfers between devices, shifted(): lax.ppermute(value, axis, [(source, source + steps) for source in range(i...  62.8 us
    all_to_all x1, waiting for transfers between devices, per_device(): lax.all_to_all(lax.all_to_all(partial_rows[None], 'req', split_axis=1, co...  31.6 us
    unnamed x31, local copies, waits for them, and re-layouts  25.2 us
    dot_general x9, matrix products, attend(): jnp.einsum('plyw,wpj->plyj', probs.astype(jnp.bfloat16), values_in_block,...  23.7 us
  transfers between devices with their start and end apart: 35, of which 28 were waited for; matrix products, arithmetic and copies ran while one was open for 10% of the time, Pallas kernels for 0%

commit v1 on v0

--- a/solution.py
+++ b/solution.py
@@ -148,12 +148,22 @@
     partial_rows = partial_out.astype(jnp.bfloat16).reshape(
         arrived.shape[0], arrived.shape[1], model_width
     )
-    returned_parts = lax.all_to_all(
-        lax.all_to_all(partial_rows[None], "req", split_axis=1, concat_axis=1, tiled=True),
-        "ffn",
-        split_axis=3,
-        concat_axis=0,
-        tiled=True,
+    returned_parts = jnp.concatenate(
+        lax.all_to_all(
+            jnp.stack(
+                jnp.split(
+                    lax.all_to_all(
+                        partial_rows[None], "req", split_axis=1, concat_axis=1, tiled=True
+                    ),
+                    lax.axis_size("ffn"),
+                    axis=3,
+                )
+            ),
+            "ffn",
+            0,
+            0,
+        ),
+        axis=0,
     )
     returned = jnp.sum(returned_parts.astype(jnp.float32), axis=0)
     expert_of = jnp.sum(dest_hot * placement[None, :], axis=1).reshape(tok_count, 2)

time: 696 us -> 650 us (0.934)
  local copies, waits for them, and re-layouts: 105 us -> 68.5 us
    all_to_all x2 -> x0, local copies, waits for them, and re-layouts: 22.2 us -> none  [the longest x1 14.3 us: per_device(): lax.all_to_all(partial_rows[None], 'req', split_axis=1, concat_axis=1, ti...]
    unnamed x31 -> x27, local copies, waits for them, and re-layouts: 25.2 us -> 11.9 us
  transfers between devices with their start and end apart: 35 -> 35, of which waited for: 28 -> 28; matrix products, arithmetic and copies ran while one was open for 10% -> 11% of each run, Pallas kernels for 0% -> 0%
where the time goes in v1:
time: 650 us; the launch traced here: 647 us
  blocking collectives  207 us (32%)
  waiting for transfers between devices  202 us (31%)
  local copies, waits for them, and re-layouts  68.5 us (11%)
  starting transfers between devices  67.7 us (10%)
  matrix products  60.8 us (9%)
  other arithmetic  25.8 us (4%)
  between operations  13.7 us (2%)
    all_to_all x1, blocking collectives, per_device(): lax.all_to_all(send_rows, 'req', split_axis=0, concat_axis=0, tiled=True)  106 us
    all_to_all x1, blocking collectives, per_device(): lax.all_to_all(partial_rows[None], 'req', split_axis=1, concat_axis=1, ti...  102 us
    ppermute x32, waiting for transfers between devices, shifted(): lax.ppermute(value, axis, [(source, source + steps) for source in range(i...  99.5 us
    psum x1, waiting for transfers between devices, per_device(): summed = lax.psum(proj.astype(jnp.bfloat16), 'ffn').astype(jnp.float32)  69.9 us
    ppermute x32, starting transfers between devices, shifted(): lax.ppermute(value, axis, [(source, source + steps) for source in range(i...  62.8 us
    all_to_all x1, waiting for transfers between devices, per_device(): lax.all_to_all(jnp.stack(jnp.split(lax.all_to_all(partial_rows[None], 're...  31.6 us
    dot_general x9, matrix products, attend(): jnp.einsum('plyw,wpj->plyj', probs.astype(jnp.bfloat16), values_in_block,...  23.7 us
    dot_general x9, matrix products, attend(): jnp.einsum('veck,uek->ecvu', shard_queries, keys_in_block, preferred_elem...  16.6 us
  transfers between devices with their start and end apart: 35, of which 28 were waited for; matrix products, arithmetic and copies ran while one was open for 11% of the time, Pallas kernels for 0%

profile of v1, /device:TPU:32, one launch (start us, length us, event | category | flops | bytes accessed | tf_op | source)
XLA Modules:
  0.0 646.8 jit_solution(13950032560015892701)
XLA Ops:
  25.7 217.2 %while.24 = (s32[]{:T(128)}, f32[4,2,256]{2,1,0:T(2,128)S(1)}, f32[4,2,256]{2,1,0:T(2,128)S(1)}, f32[4,2,256,128]{3,2,1,0:T(8,128)}, bf16[256,4,128]{2,0,1:T(8,1...) while((s32[]{:T(128)}, f32[4,2,256]{2,1,0:T(2,128)S(1)}, ...), condition=%wide.region_5.6_spmd.clone, body=%wide.region_2.5_spmd.clone.sunk | while | flops 551817984 | bytes 30547376 | solution.py:111
  27.6 3.5 collective-permute-start.2
  31.2 4.8 collective-permute-done
  41.2 5.1 collective-permute-done.1
  57.1 6.0 collective-permute-done
  69.4 5.7 collective-permute-done.1
  87.7 6.0 collective-permute-done
  98.4 5.3 collective-permute-done.1
  114.2 6.0 collective-permute-done
  124.9 5.3 collective-permute-done.1
  140.7 6.0 collective-permute-done
  151.5 5.3 collective-permute-done.1
  167.2 6.0 collective-permute-done
  178.0 5.3 collective-permute-done.1
  193.7 6.0 collective-permute-done
  204.5 5.3 collective-permute-done.1
  220.3 6.0 collective-permute-done
  231.0 5.3 collective-permute-done.1
  247.6 4.7 convolution_convert_fusion.1
  254.4 69.9 %all-reduce.2.cloned.1.call-done = bf16[256,2048]{1,0:T(8,128)(2,1)} async-done(((bf16[256,2048]{1,0:T(8,128)(2,1)}), bf16[256,2048]{1,0:T(8,128)(2,1)}) %all-reduce.2.cloned.1.call-update) | async-done | bytes 1048592 | tf_op jit(solution)/shard_map/psum | solution.py:122
  324.4 3.4 convert_add_fusion
  329.3 11.3 %scatter_custom_fusion = bf16[640,2048]{1,0:T(8,128)(2,1)} fusion(s32[512]{0:T(512)S(1)} %bitcast.140, bf16[256,2048]{1,0:T(8,128)(2,1)} %multiply_convert_fusion, s32[1024]{0:T(1024)S(1)} %pad_clamp_fusion.1, bf16[]{:T(256)} %constant.128.clone.1), kind=kCustom, calls=%fused_computation.42 | custom fusion | bytes 2621952 | tf_op jit(solution)/shard_map/scatter | solution.py:137
  340.6 5.4 reshape.362
  346.0 105.9 %all_to_all.15 = bf16[64,10,2048]{2,1,0:T(8,128)(2,1)} all-to-all(bf16[64,10,2048]{2,1,0:T(8,128)(2,1)} %reshape.362), channel_id=1, replica_groups=mesh['req'=64,'ffn'=4] {'req'}, dimensions={0} | all-to-all | bytes 5242880 | tf_op jit(solution)/shard_map/all_to_all | solution.py:140
  451.9 5.5 reshape.363
  457.4 6.2 fusion.27
  463.6 9.7 %convolution_convert_fusion = bf16[640,2048]{1,0:T(8,128)(2,1)} fusion(bf16[1,2048,768]{2,1,0:T(8,128)(2,1)S(1)} %copy-done, f32[640,768]{1,0:T(8,128)} %fusion.27, bf16[640,2048]{1,0:T(8,128)(2,1)} %reshape.363, bf16[1,2048,768]{2,1,0:T(8,128)(2,1)} %param.28), kind=kOutput, calls=%fused_computation.34 | convolution fusion | flops 4030791680 | bytes 13500416 | tf_op jit(solution)/shard_map/dot_general | solution.py:145
  473.3 5.4 broadcast_in_dim_reshape.2
  478.7 101.6 %all_to_all.16 = bf16[1,64,10,2048]{3,2,0,1:T(8,128)(2,1)S(1)} all-to-all(bf16[1,64,10,2048]{3,2,0,1:T(8,128)(2,1)} %bitcast.125), channel_id=1, replica_groups=mesh['req'=64,'ffn'=4] {'req'}, dimensions={1} | all-to-all | bytes 5242880 | tf_op jit(solution)/shard_map/all_to_all | solution.py:155
  584.6 4.9 all-to-all-start.2
  590.1 31.6 %all-to-all-done.2 = bf16[4,1,64,10,512]{4,2,3,1,0:T(8,128)(2,1)} async-done(((bf16[4,1,64,10,512]{4,2,3,1,0:T(8,128)(2,1)}), bf16[4,1,64,10,512]{4,2,3,1,0:T(8,128)(2,1)}, u32[]{:S(2)}, u32[]{:S(2)}) %all-to-all-start.2) | async-done | bytes 2621472 | tf_op jit(solution)/shard_map/all_to_all | solution.py:152
  628.7 4.0 gather_fusion
  (243 shorter events, 169.5 us)
Async XLA Ops:
  6.5 241.1 %all-gather.2.cloned.1.call-start = ((), (), s32[]{:S(2)}) async-start(), calls=%async_computation.3 | async-start | bytes 4259840 | tf_op jit(solution)/shard_map/all_gather | solution.py:119
  7.3 317.1 %all-reduce.2.cloned.1.call-start = ((), (), s32[]{:S(2)}) async-start(), calls=%async_computation.4 | async-start | bytes 2097152 | tf_op jit(solution)/shard_map/psum | solution.py:122
  25.7 10.2 %collective-permute-start = (bf16[256,4,128]{2,0,1:T(8,128)(2,1)S(1)}, bf16[256,4,128]{2,0,1:T(8,128)(2,1)}, u32[]{:S(2)}, u32[]{:S(2)}) collective-permute-start(bf16[256,4,128]{2,0,1:T(8,128)(2,1)S(1)} %get-tuple-element.439), channel_id=1, source_target_pairs={{0,4},{4,8},{8,12},{12,16},{16,20},{20,24},{24,28},{28,32},{32,36}... | collective-permute-start | bytes 786440 | tf_op jit(solution)/shard_map/while/body/eval_jaxpr/ppermute | solution.py:16
  27.6 11.7 %collective-permute-start.2 = (bf16[256,4,128]{2,0,1:T(8,128)(2,1)}, bf16[256,4,128]{2,0,1:T(8,128)(2,1)}, u32[]{:S(2)}, u32[]{:S(2)}) collective-permute-start(bf16[256,4,128]{2,0,1:T(8,128)(2,1)} %get-tuple-element.440), channel_id=1, source_target_pairs={{0,4},{4,8},{8,12},{12,16},{16,20},{20,24},{24,28},{28,32},{32,36}... | collective-permute-start | bytes 786440 | tf_op jit(solution)/shard_map/while/body/eval_jaxpr/ppermute | solution.py:16
  36.0 10.4 %collective-permute-start.1 = (bf16[256,4,128]{2,0,1:T(8,128)(2,1)}, bf16[256,4,128]{2,0,1:T(8,128)(2,1)S(1)}, u32[]{:S(2)}, u32[]{:S(2)}) collective-permute-start(bf16[256,4,128]{2,0,1:T(8,128)(2,1)} %collective-permute-done), channel_id=1, source_target_pairs={{0,4},{4,8},{8,12},{12,16},{16,20},{20,24},{24,28},{28,32},{32,36}... | collective-permute-start | bytes 786440 | tf_op jit(solution)/shard_map/while/body/eval_jaxpr/ppermute | solution.py:16
  39.3 10.3 %collective-permute-start.3 = (bf16[256,4,128]{2,0,1:T(8,128)(2,1)}, bf16[256,4,128]{2,0,1:T(8,128)(2,1)S(1)}, u32[]{:S(2)}, u32[]{:S(2)}) collective-permute-start(bf16[256,4,128]{2,0,1:T(8,128)(2,1)} %collective-permute-done.2), channel_id=1, source_target_pairs={{0,4},{4,8},{8,12},{12,16},{16,20},{20,24},{24,28},{28,32},{32,36}... | collective-permute-start | bytes 786440 | tf_op jit(solution)/shard_map/while/body/eval_jaxpr/ppermute | solution.py:16
  53.3 9.9 %collective-permute-start = (bf16[256,4,128]{2,0,1:T(8,128)(2,1)S(1)}, bf16[256,4,128]{2,0,1:T(8,128)(2,1)}, u32[]{:S(2)}, u32[]{:S(2)}) collective-permute-start(bf16[256,4,128]{2,0,1:T(8,128)(2,1)S(1)} %get-tuple-element.439), channel_id=1, source_target_pairs={{0,4},{4,8},{8,12},{12,16},{16,20},{20,24},{24,28},{28,32},{32,36}... | collective-permute-start | bytes 786440 | tf_op jit(solution)/shard_map/while/body/eval_jaxpr/ppermute | solution.py:16
  55.2 12.3 %collective-permute-start.2 = (bf16[256,4,128]{2,0,1:T(8,128)(2,1)}, bf16[256,4,128]{2,0,1:T(8,128)(2,1)}, u32[]{:S(2)}, u32[]{:S(2)}) collective-permute-start(bf16[256,4,128]{2,0,1:T(8,128)(2,1)} %get-tuple-element.440), channel_id=1, source_target_pairs={{0,4},{4,8},{8,12},{12,16},{16,20},{20,24},{24,28},{28,32},{32,36}... | collective-permute-start | bytes 786440 | tf_op jit(solution)/shard_map/while/body/eval_jaxpr/ppermute | solution.py:16
  63.2 11.9 %collective-permute-start.1 = (bf16[256,4,128]{2,0,1:T(8,128)(2,1)}, bf16[256,4,128]{2,0,1:T(8,128)(2,1)S(1)}, u32[]{:S(2)}, u32[]{:S(2)}) collective-permute-start(bf16[256,4,128]{2,0,1:T(8,128)(2,1)} %collective-permute-done), channel_id=1, source_target_pairs={{0,4},{4,8},{8,12},{12,16},{16,20},{20,24},{24,28},{28,32},{32,36}... | collective-permute-start | bytes 786440 | tf_op jit(solution)/shard_map/while/body/eval_jaxpr/ppermute | solution.py:16
  67.5 12.7 %collective-permute-start.3 = (bf16[256,4,128]{2,0,1:T(8,128)(2,1)}, bf16[256,4,128]{2,0,1:T(8,128)(2,1)S(1)}, u32[]{:S(2)}, u32[]{:S(2)}) collective-permute-start(bf16[256,4,128]{2,0,1:T(8,128)(2,1)} %collective-permute-done.2), channel_id=1, source_target_pairs={{0,4},{4,8},{8,12},{12,16},{16,20},{20,24},{24,28},{28,32},{32,36}... | collective-permute-start | bytes 786440 | tf_op jit(solution)/shard_map/while/body/eval_jaxpr/ppermute | solution.py:16
  83.8 9.9 %collective-permute-start = (bf16[256,4,128]{2,0,1:T(8,128)(2,1)S(1)}, bf16[256,4,128]{2,0,1:T(8,128)(2,1)}, u32[]{:S(2)}, u32[]{:S(2)}) collective-permute-start(bf16[256,4,128]{2,0,1:T(8,128)(2,1)S(1)} %get-tuple-element.439), channel_id=1, source_target_pairs={{0,4},{4,8},{8,12},{12,16},{16,20},{20,24},{24,28},{28,32},{32,36}... | collective-permute-start | bytes 786440 | tf_op jit(solution)/shard_map/while/body/eval_jaxpr/ppermute | solution.py:16
  85.7 10.8 %collective-permute-start.2 = (bf16[256,4,128]{2,0,1:T(8,128)(2,1)}, bf16[256,4,128]{2,0,1:T(8,128)(2,1)}, u32[]{:S(2)}, u32[]{:S(2)}) collective-permute-start(bf16[256,4,128]{2,0,1:T(8,128)(2,1)} %get-tuple-element.440), channel_id=1, source_target_pairs={{0,4},{4,8},{8,12},{12,16},{16,20},{20,24},{24,28},{28,32},{32,36}... | collective-permute-start | bytes 786440 | tf_op jit(solution)/shard_map/while/body/eval_jaxpr/ppermute | solution.py:16
  93.7 10.0 %collective-permute-start.1 = (bf16[256,4,128]{2,0,1:T(8,128)(2,1)}, bf16[256,4,128]{2,0,1:T(8,128)(2,1)S(1)}, u32[]{:S(2)}, u32[]{:S(2)}) collective-permute-start(bf16[256,4,128]{2,0,1:T(8,128)(2,1)} %collective-permute-done), channel_id=1, source_target_pairs={{0,4},{4,8},{8,12},{12,16},{16,20},{20,24},{24,28},{28,32},{32,36}... | collective-permute-start | bytes 786440 | tf_op jit(solution)/shard_map/while/body/eval_jaxpr/ppermute | solution.py:16
  96.5 10.0 %collective-permute-start.3 = (bf16[256,4,128]{2,0,1:T(8,128)(2,1)}, bf16[256,4,128]{2,0,1:T(8,128)(2,1)S(1)}, u32[]{:S(2)}, u32[]{:S(2)}) collective-permute-start(bf16[256,4,128]{2,0,1:T(8,128)(2,1)} %collective-permute-done.2), channel_id=1, source_target_pairs={{0,4},{4,8},{8,12},{12,16},{16,20},{20,24},{24,28},{28,32},{32,36}... | collective-permute-start | bytes 786440 | tf_op jit(solution)/shard_map/while/body/eval_jaxpr/ppermute | solution.py:16
  110.3 9.9 %collective-permute-start = (bf16[256,4,128]{2,0,1:T(8,128)(2,1)S(1)}, bf16[256,4,128]{2,0,1:T(8,128)(2,1)}, u32[]{:S(2)}, u32[]{:S(2)}) collective-permute-start(bf16[256,4,128]{2,0,1:T(8,128)(2,1)S(1)} %get-tuple-element.439), channel_id=1, source_target_pairs={{0,4},{4,8},{8,12},{12,16},{16,20},{20,24},{24,28},{28,32},{32,36}... | collective-permute-start | bytes 786440 | tf_op jit(solution)/shard_map/while/body/eval_jaxpr/ppermute | solution.py:16
  112.2 10.8 %collective-permute-start.2 = (bf16[256,4,128]{2,0,1:T(8,128)(2,1)}, bf16[256,4,128]{2,0,1:T(8,128)(2,1)}, u32[]{:S(2)}, u32[]{:S(2)}) collective-permute-start(bf16[256,4,128]{2,0,1:T(8,128)(2,1)} %get-tuple-element.440), channel_id=1, source_target_pairs={{0,4},{4,8},{8,12},{12,16},{16,20},{20,24},{24,28},{28,32},{32,36}... | collective-permute-start | bytes 786440 | tf_op jit(solution)/shard_map/while/body/eval_jaxpr/ppermute | solution.py:16
  120.2 10.0 %collective-permute-start.1 = (bf16[256,4,128]{2,0,1:T(8,128)(2,1)}, bf16[256,4,128]{2,0,1:T(8,128)(2,1)S(1)}, u32[]{:S(2)}, u32[]{:S(2)}) collective-permute-start(bf16[256,4,128]{2,0,1:T(8,128)(2,1)} %collective-permute-done), channel_id=1, source_target_pairs={{0,4},{4,8},{8,12},{12,16},{16,20},{20,24},{24,28},{28,32},{32,36}... | collective-permute-start | bytes 786440 | tf_op jit(solution)/shard_map/while/body/eval_jaxpr/ppermute | solution.py:16
  123.0 10.0 %collective-permute-start.3 = (bf16[256,4,128]{2,0,1:T(8,128)(2,1)}, bf16[256,4,128]{2,0,1:T(8,128)(2,1)S(1)}, u32[]{:S(2)}, u32[]{:S(2)}) collective-permute-start(bf16[256,4,128]{2,0,1:T(8,128)(2,1)} %collective-permute-done.2), channel_id=1, source_target_pairs={{0,4},{4,8},{8,12},{12,16},{16,20},{20,24},{24,28},{28,32},{32,36}... | collective-permute-start | bytes 786440 | tf_op jit(solution)/shard_map/while/body/eval_jaxpr/ppermute | solution.py:16
  136.8 9.9 %collective-permute-start = (bf16[256,4,128]{2,0,1:T(8,128)(2,1)S(1)}, bf16[256,4,128]{2,0,1:T(8,128)(2,1)}, u32[]{:S(2)}, u32[]{:S(2)}) collective-permute-start(bf16[256,4,128]{2,0,1:T(8,128)(2,1)S(1)} %get-tuple-element.439), channel_id=1, source_target_pairs={{0,4},{4,8},{8,12},{12,16},{16,20},{20,24},{24,28},{28,32},{32,36}... | collective-permute-start | bytes 786440 | tf_op jit(solution)/shard_map/while/body/eval_jaxpr/ppermute | solution.py:16
  138.8 10.8 %collective-permute-start.2 = (bf16[256,4,128]{2,0,1:T(8,128)(2,1)}, bf16[256,4,128]{2,0,1:T(8,128)(2,1)}, u32[]{:S(2)}, u32[]{:S(2)}) collective-permute-start(bf16[256,4,128]{2,0,1:T(8,128)(2,1)} %get-tuple-element.440), channel_id=1, source_target_pairs={{0,4},{4,8},{8,12},{12,16},{16,20},{20,24},{24,28},{28,32},{32,36}... | collective-permute-start | bytes 786440 | tf_op jit(solution)/shard_map/while/body/eval_jaxpr/ppermute | solution.py:16
  146.7 10.0 %collective-permute-start.1 = (bf16[256,4,128]{2,0,1:T(8,128)(2,1)}, bf16[256,4,128]{2,0,1:T(8,128)(2,1)S(1)}, u32[]{:S(2)}, u32[]{:S(2)}) collective-permute-start(bf16[256,4,128]{2,0,1:T(8,128)(2,1)} %collective-permute-done), channel_id=1, source_target_pairs={{0,4},{4,8},{8,12},{12,16},{16,20},{20,24},{24,28},{28,32},{32,36}... | collective-permute-start | bytes 786440 | tf_op jit(solution)/shard_map/while/body/eval_jaxpr/ppermute | solution.py:16
  149.6 10.0 %collective-permute-start.3 = (bf16[256,4,128]{2,0,1:T(8,128)(2,1)}, bf16[256,4,128]{2,0,1:T(8,128)(2,1)S(1)}, u32[]{:S(2)}, u32[]{:S(2)}) collective-permute-start(bf16[256,4,128]{2,0,1:T(8,128)(2,1)} %collective-permute-done.2), channel_id=1, source_target_pairs={{0,4},{4,8},{8,12},{12,16},{16,20},{20,24},{24,28},{28,32},{32,36}... | collective-permute-start | bytes 786440 | tf_op jit(solution)/shard_map/while/body/eval_jaxpr/ppermute | solution.py:16
  165.3 10.8 %collective-permute-start.2 = (bf16[256,4,128]{2,0,1:T(8,128)(2,1)}, bf16[256,4,128]{2,0,1:T(8,128)(2,1)}, u32[]{:S(2)}, u32[]{:S(2)}) collective-permute-start(bf16[256,4,128]{2,0,1:T(8,128)(2,1)} %get-tuple-element.440), channel_id=1, source_target_pairs={{0,4},{4,8},{8,12},{12,16},{16,20},{20,24},{24,28},{28,32},{32,36}... | collective-permute-start | bytes 786440 | tf_op jit(solution)/shard_map/while/body/eval_jaxpr/ppermute | solution.py:16
  173.3 10.0 %collective-permute-start.1 = (bf16[256,4,128]{2,0,1:T(8,128)(2,1)}, bf16[256,4,128]{2,0,1:T(8,128)(2,1)S(1)}, u32[]{:S(2)}, u32[]{:S(2)}) collective-permute-start(bf16[256,4,128]{2,0,1:T(8,128)(2,1)} %collective-permute-done), channel_id=1, source_target_pairs={{0,4},{4,8},{8,12},{12,16},{16,20},{20,24},{24,28},{28,32},{32,36}... | collective-permute-start | bytes 786440 | tf_op jit(solution)/shard_map/while/body/eval_jaxpr/ppermute | solution.py:16
  176.1 10.0 %collective-permute-start.3 = (bf16[256,4,128]{2,0,1:T(8,128)(2,1)}, bf16[256,4,128]{2,0,1:T(8,128)(2,1)S(1)}, u32[]{:S(2)}, u32[]{:S(2)}) collective-permute-start(bf16[256,4,128]{2,0,1:T(8,128)(2,1)} %collective-permute-done.2), channel_id=1, source_target_pairs={{0,4},{4,8},{8,12},{12,16},{16,20},{20,24},{24,28},{28,32},{32,36}... | collective-permute-start | bytes 786440 | tf_op jit(solution)/shard_map/while/body/eval_jaxpr/ppermute | solution.py:16
  191.8 10.8 %collective-permute-start.2 = (bf16[256,4,128]{2,0,1:T(8,128)(2,1)}, bf16[256,4,128]{2,0,1:T(8,128)(2,1)}, u32[]{:S(2)}, u32[]{:S(2)}) collective-permute-start(bf16[256,4,128]{2,0,1:T(8,128)(2,1)} %get-tuple-element.440), channel_id=1, source_target_pairs={{0,4},{4,8},{8,12},{12,16},{16,20},{20,24},{24,28},{28,32},{32,36}... | collective-permute-start | bytes 786440 | tf_op jit(solution)/shard_map/while/body/eval_jaxpr/ppermute | solution.py:16
  199.8 10.0 %collective-permute-start.1 = (bf16[256,4,128]{2,0,1:T(8,128)(2,1)}, bf16[256,4,128]{2,0,1:T(8,128)(2,1)S(1)}, u32[]{:S(2)}, u32[]{:S(2)}) collective-permute-start(bf16[256,4,128]{2,0,1:T(8,128)(2,1)} %collective-permute-done), channel_id=1, source_target_pairs={{0,4},{4,8},{8,12},{12,16},{16,20},{20,24},{24,28},{28,32},{32,36}... | collective-permute-start | bytes 786440 | tf_op jit(solution)/shard_map/while/body/eval_jaxpr/ppermute | solution.py:16
  202.6 10.0 %collective-permute-start.3 = (bf16[256,4,128]{2,0,1:T(8,128)(2,1)}, bf16[256,4,128]{2,0,1:T(8,128)(2,1)S(1)}, u32[]{:S(2)}, u32[]{:S(2)}) collective-permute-start(bf16[256,4,128]{2,0,1:T(8,128)(2,1)} %collective-permute-done.2), channel_id=1, source_target_pairs={{0,4},{4,8},{8,12},{12,16},{16,20},{20,24},{24,28},{28,32},{32,36}... | collective-permute-start | bytes 786440 | tf_op jit(solution)/shard_map/while/body/eval_jaxpr/ppermute | solution.py:16
  218.3 10.8 %collective-permute-start.2 = (bf16[256,4,128]{2,0,1:T(8,128)(2,1)}, bf16[256,4,128]{2,0,1:T(8,128)(2,1)}, u32[]{:S(2)}, u32[]{:S(2)}) collective-permute-start(bf16[256,4,128]{2,0,1:T(8,128)(2,1)} %get-tuple-element.440), channel_id=1, source_target_pairs={{0,4},{4,8},{8,12},{12,16},{16,20},{20,24},{24,28},{28,32},{32,36}... | collective-permute-start | bytes 786440 | tf_op jit(solution)/shard_map/while/body/eval_jaxpr/ppermute | solution.py:16
  226.3 10.0 %collective-permute-start.1 = (bf16[256,4,128]{2,0,1:T(8,128)(2,1)}, bf16[256,4,128]{2,0,1:T(8,128)(2,1)S(1)}, u32[]{:S(2)}, u32[]{:S(2)}) collective-permute-start(bf16[256,4,128]{2,0,1:T(8,128)(2,1)} %collective-permute-done), channel_id=1, source_target_pairs={{0,4},{4,8},{8,12},{12,16},{16,20},{20,24},{24,28},{28,32},{32,36}... | collective-permute-start | bytes 786440 | tf_op jit(solution)/shard_map/while/body/eval_jaxpr/ppermute | solution.py:16
  229.1 10.0 %collective-permute-start.3 = (bf16[256,4,128]{2,0,1:T(8,128)(2,1)}, bf16[256,4,128]{2,0,1:T(8,128)(2,1)S(1)}, u32[]{:S(2)}, u32[]{:S(2)}) collective-permute-start(bf16[256,4,128]{2,0,1:T(8,128)(2,1)} %collective-permute-done.2), channel_id=1, source_target_pairs={{0,4},{4,8},{8,12},{12,16},{16,20},{20,24},{24,28},{28,32},{32,36}... | collective-permute-start | bytes 786440 | tf_op jit(solution)/shard_map/while/body/eval_jaxpr/ppermute | solution.py:16
  584.6 37.1 %all-to-all-start.2 = ((bf16[4,1,64,10,512]{4,2,3,1,0:T(8,128)(2,1)}), bf16[4,1,64,10,512]{4,2,3,1,0:T(8,128)(2,1)}, u32[]{:S(2)}, u32[]{:S(2)}) async-start(bf16[4,1,64,10,512]{4,2,3,1,0:T(8,128)(2,1)} %copy.100), calls=%async_computation.2 | async-start | bytes 5242880 | tf_op jit(solution)/shard_map/all_to_all | solution.py:152
  (37 other events, 643.7 us)
Sparse Core Ops, SparseCore 0:
  10.1 83.0 all-gather.1
  252.4 71.9 all-reduce.1
